TPU v7x, 512 devices: a whole 4x4x16 slice. The times are simulated.
512 devices in a mesh: dp: 8 (over y, x_hi), context: 64 (over x_lo, z, core).
Axes of the slice: x: 4 (x_hi: 2, x_lo: 2; x = x_hi * 2 + x_lo), y: 4, z: 16, core: 2. Of those that a mesh axis runs over, the one named last changes fastest.
Arguments:
- codes: int32 [8, 65536], P('dp', 'context'), may hold values from 0 to 3
- variant_pos: int32 [8, 64], P('dp'), may hold values from 0 to 65535
- variant_shift: int32 [8, 64], P('dp'), may hold values from 1 to 3
- stem_weight: float32 [15, 4, 384], replicated, may hold values from -1.5 to 1.5
- conv_weight: bfloat16 [5, 384, 384], replicated, may hold values from -0.125 to 0.125
- cotangent: bfloat16 [8, 32768, 384], P('dp', 'context'), may hold values from -6 to 6
Outputs:
- features: bfloat16 [8, 32768, 384], P('dp', 'context')
- d_pooled: bfloat16 [8, 32768, 384], P('dp', 'context')
- conv_grad: float32 [5, 384, 384], replicated
- stem_grad: float32 [15, 4, 384], replicated
All inputs are finite; a program needn't handle non-finite values.
Results may differ from a plain program's by a relative error of at most 0.009.
Values may be sent and summed in bfloat16 or wider, within the bound.
A program may use at most 64 MiB of HBM per device.

v0:
```python
import math
import jax
import jax.numpy as jnp
from jax import lax
from jax.sharding import PartitionSpec as P

root_scale = math.sqrt(2.0 / math.pi)
cubic = 0.044715


def with_halo(block, sides, width):
    for axis, dim in sides:
        count = lax.axis_size(axis)
        forward = [(i, i + 1) for i in range(count - 1)]
        backward = [(target, source) for source, target in forward]
        low = lax.ppermute(
            lax.slice_in_dim(block, block.shape[dim] - width, None, axis=dim), axis, forward
        )
        high = lax.ppermute(lax.slice_in_dim(block, 0, width, axis=dim), axis, backward)
        block = jnp.concatenate([low, block, high], axis=dim)
    return block


def gelu_tanh(value):
    return 0.5 * value * (1.0 + jnp.tanh(root_scale * (value + cubic * value * value * value)))


def gelu_slope(value):
    inner = jnp.tanh(root_scale * (value + cubic * value * value * value))
    return 0.5 * (1.0 + inner) + 0.5 * value * (1.0 - inner * inner) * root_scale * (
        1.0 + 3.0 * cubic * value * value
    )


def per_device(codes, variant_pos, variant_shift, stem_weight, conv_weight, cotangent):
    length = codes.shape[1]
    half_rows = length // 2
    width = stem_weight.shape[2]
    first_base = lax.axis_index("context") * length
    places = first_base + jnp.arange(length, dtype=jnp.int32)
    matches = (variant_pos[:, None, :] == places[None, :, None]).astype(jnp.int32)
    shifts = jnp.sum(matches * variant_shift[:, None, :], axis=2)
    mutated = (codes + shifts) % 4 + 1
    extended = with_halo(mutated, (("context", 1),), 7)
    onehot = (extended[:, :, None] == jnp.arange(1, 5, dtype=jnp.int32)[None, None, :]).astype(
        jnp.float32
    )
    windows = jnp.concatenate([onehot[:, k : k + length] for k in range(15)], axis=2)
    flat_stem = stem_weight.reshape(60, width)
    stem = jnp.einsum(
        "blk,kc->blc",
        windows,
        flat_stem,
        precision=lax.Precision.HIGHEST,
        preferred_element_type=jnp.float32,
    )
    active = gelu_tanh(stem)
    pooled = (0.5 * (active[:, 0::2] + active[:, 1::2])).astype(jnp.bfloat16)
    pooled_f = pooled.astype(jnp.float32)
    gated = gelu_tanh(pooled_f).astype(jnp.bfloat16)
    gated_ext = with_halo(gated, (("context", 1),), 2)
    cot_ext = with_halo(cotangent, (("context", 1),), 2)
    conv_out = jnp.zeros((gated.shape[0], half_rows, width), jnp.float32)
    back = jnp.zeros((gated.shape[0], half_rows, width), jnp.float32)
    for offset in range(5):
        conv_out = conv_out + jnp.einsum(
            "brc,cd->brd",
            gated_ext[:, offset : offset + half_rows],
            conv_weight[offset],
            preferred_element_type=jnp.float32,
        )
        back = back + jnp.einsum(
            "brd,cd->brc",
            cot_ext[:, 4 - offset : 4 - offset + half_rows],
            conv_weight[offset],
            preferred_element_type=jnp.float32,
        )
    features = (pooled_f + conv_out).astype(jnp.bfloat16)
    dpool = cotangent.astype(jnp.float32) + back * gelu_slope(pooled_f)
    d_pooled = dpool.astype(jnp.bfloat16)
    tap_grads = jnp.stack(
        [
            jnp.einsum(
                "brc,brd->cd",
                gated_ext[:, offset : offset + half_rows],
                cotangent,
                preferred_element_type=jnp.float32,
            )
            for offset in range(5)
        ]
    )
    dstem = 0.5 * jnp.repeat(dpool, 2, axis=1) * gelu_slope(stem)
    stem_part = jnp.einsum(
        "blk,blc->kc",
        windows,
        dstem,
        precision=lax.Precision.HIGHEST,
        preferred_element_type=jnp.float32,
    )
    stem_grad = lax.psum(stem_part, ("dp", "context")).reshape(15, 4, width)
    conv_grad = lax.psum(tap_grads, ("dp", "context"))
    return (features, d_pooled, conv_grad, stem_grad)


def solution(mesh):
    placed = (P("dp", "context"), P("dp", None), P("dp", None), P(), P(), P("dp", "context", None))
    return jax.shard_map(
        per_device,
        mesh=mesh,
        in_specs=placed,
        out_specs=(P("dp", "context", None), P("dp", "context", None), P(), P()),
        check_vma=False,
    )
```

profile of v0, /device:TPU:2, one launch (start us, length us, event | category | flops | bytes accessed | tf_op | source)
XLA Modules:
  0.0 567.2 jit_solution(724238133295681119)
XLA Ops:
  7.2 0.8 select_reduce_fusion
  8.0 0.7 fusion.93
  8.8 10.8 %collective-permute-start.1 = (s32[1,7]{1,0:T(1,128)S(1)}, s32[1,7]{1,0:T(1,128)S(1)}, u32[]{:S(2)}, u32[]{:S(2)}) collective-permute-start(s32[1,7]{1,0:T(1,128)S(1)} %get-tuple-element.14), channel_id=1, source_target_pairs={{1,0},{2,1},{3,2},{4,3},{5,4},{6,5},{7,6},{8,7},{9,8},{10,9},{11,1... | collective-permute-start | bytes 92 | tf_op jit(solution)/shard_map/ppermute | solution.py:19
  19.6 1.9 collective-permute-start
  21.5 1.3 fusion.112
  22.8 1.9 collective-permute-start.5
  24.7 5.8 %collective-permute-start.4 = (bf16[1,2,384]{2,1,0:T(2,128)(2,1)}, bf16[1,2,384]{2,1,0:T(2,128)(2,1)S(1)}, u32[]{:S(2)}, u32[]{:S(2)}) collective-permute-start(bf16[1,2,384]{2,1,0:T(2,128)(2,1)} %get-tuple-element.11), channel_id=1, source_target_pairs={{1,0},{2,1},{3,2},{4,3},{5,4},{6,5},{7,6},{8,7},{9,8},{10,9},{11,1... | collective-permute-start | bytes 4616 | tf_op jit(solution)/shard_map/ppermute | solution.py:19
  30.5 1.8 constant_dynamic-update-slice_fusion.16
  32.3 0.9 reshape.259
  33.2 2.4 fusion.59
  37.4 1.5 fusion.75
  39.3 2.8 slice.143
  42.1 2.8 slice.142
  44.9 1.9 fusion.29
  46.7 0.6 fusion.113
  47.4 2.4 collective-permute-start.3
  49.8 2.1 collective-permute-start.2
  53.8 1.6 multiply_bitcast_fusion.1
  55.4 0.5 broadcast_in_dim.2
  55.9 2.2 mul.172
  58.2 3.6 fusion.6
  61.8 0.7 reshape.270
  62.4 1.2 fusion.25
  63.7 1.2 fusion.24
  64.9 1.3 fusion.23
  66.2 1.2 fusion.22
  67.4 1.2 fusion.21
  68.7 1.3 copy-done.1
  71.7 1.1 fusion.20
  72.8 483.2 %all-reduce.3.cloned.1.call-done = (f32[5,384,384]{2,1,0:T(8,128)}, f32[15,4,384]{2,1,0:T(4,128)}) async-done(((f32[5,384,384]{2,1,0:T(8,128)}, f32[15,4,384]{2,1,0:T(4,128)}), (f32[5,384,384]{2,1,0:T(8,128)}, f32[15,4,384]{2,1,0:T(4,128)})) %all-reduce.3.cloned.1.call-update) | async-done | bytes 3041296 | tf_op jit(solution)/shard_map/psum | solution.py:101
  556.0 3.7 copy.40
  559.7 0.6 copy.41
  (57 shorter events, 5.7 us)
Async XLA Ops:
  7.2 548.9 %all-reduce.3.cloned.1.call-start = ((), (), s32[]{:S(2)}) async-start(), calls=%async_computation | async-start | bytes 6082560 | tf_op jit(solution)/shard_map/psum | solution.py:101
  8.8 26.8 %collective-permute-start.1 = (s32[1,7]{1,0:T(1,128)S(1)}, s32[1,7]{1,0:T(1,128)S(1)}, u32[]{:S(2)}, u32[]{:S(2)}) collective-permute-start(s32[1,7]{1,0:T(1,128)S(1)} %get-tuple-element.14), channel_id=1, source_target_pairs={{1,0},{2,1},{3,2},{4,3},{5,4},{6,5},{7,6},{8,7},{9,8},{10,9},{11,1... | collective-permute-start | bytes 92 | tf_op jit(solution)/shard_map/ppermute | solution.py:19
  19.6 16.0 %collective-permute-start = (s32[1,7]{1,0:T(1,128)S(1)}, s32[1,7]{1,0:T(1,128)S(1)}, u32[]{:S(2)}, u32[]{:S(2)}) collective-permute-start(s32[1,7]{1,0:T(1,128)S(1)} %get-tuple-element.15), channel_id=1, source_target_pairs={{0,1},{1,2},{2,3},{3,4},{4,5},{5,6},{6,7},{7,8},{8,9},{9,10},{10,1... | collective-permute-start | bytes 92 | tf_op jit(solution)/shard_map/ppermute | solution.py:16
  22.8 30.0 %collective-permute-start.5 = (bf16[1,2,384]{2,1,0:T(2,128)(2,1)}, bf16[1,2,384]{2,1,0:T(2,128)(2,1)S(1)}, u32[]{:S(2)}, u32[]{:S(2)}) collective-permute-start(bf16[1,2,384]{2,1,0:T(2,128)(2,1)} %get-tuple-element.10), channel_id=1, source_target_pairs={{0,1},{1,2},{2,3},{3,4},{4,5},{5,6},{6,7},{7,8},{8,9},{9,10},{10,1... | collective-permute-start | bytes 4616 | tf_op jit(solution)/shard_map/ppermute | solution.py:16
  24.7 27.2 %collective-permute-start.4 = (bf16[1,2,384]{2,1,0:T(2,128)(2,1)}, bf16[1,2,384]{2,1,0:T(2,128)(2,1)S(1)}, u32[]{:S(2)}, u32[]{:S(2)}) collective-permute-start(bf16[1,2,384]{2,1,0:T(2,128)(2,1)} %get-tuple-element.11), channel_id=1, source_target_pairs={{1,0},{2,1},{3,2},{4,3},{5,4},{6,5},{7,6},{8,7},{9,8},{10,9},{11,1... | collective-permute-start | bytes 4616 | tf_op jit(solution)/shard_map/ppermute | solution.py:19
  37.4 1.9 copy-start.8
  44.8 7.1 %copy-start.4 = (bf16[1,514,384]{2,1,0:T(8,128)(2,1)S(1)}, bf16[1,514,384]{2,1,0:T(8,128)(2,1)}, u32[]{:S(2)}) copy-start(bf16[1,514,384]{2,1,0:T(8,128)(2,1)} %constant_dynamic-update-slice_fusion.16) | copy-start | bytes 1184260
  44.9 7.1 %copy-start = (bf16[5,384,384]{2,1,0:T(8,128)(2,1)S(1)}, bf16[5,384,384]{2,1,0:T(8,128)(2,1)}, u32[]{:S(2)}) copy-start(bf16[5,384,384]{2,1,0:T(8,128)(2,1)} %param.10) | copy-start | bytes 4423684
  44.9 7.5 %copy-start.5 = (f32[512,384]{1,0:T(8,128)S(1)}, f32[512,384]{1,0:T(8,128)}, u32[]{:S(2)}) copy-start(f32[512,384]{1,0:T(8,128)} %fusion.59) | copy-start | bytes 2359300
  46.7 7.1 %copy-start.6 = (bf16[1,512,384]{2,1,0:T(8,128)(2,1)}, bf16[1,512,384]{2,1,0:T(8,128)(2,1)S(1)}, u32[]{:S(2)}) copy-start(bf16[1,512,384]{2,1,0:T(8,128)(2,1)S(1)} %get-tuple-element.7) | copy-start | bytes 1179652
  47.4 18.8 %collective-permute-start.3 = (bf16[1,2,384]{2,1,0:T(2,128)(2,1)}, bf16[1,2,384]{2,1,0:T(2,128)(2,1)S(1)}, u32[]{:S(2)}, u32[]{:S(2)}) collective-permute-start(bf16[1,2,384]{2,1,0:T(2,128)(2,1)} %get-tuple-element.12), channel_id=1, source_target_pairs={{1,0},{2,1},{3,2},{4,3},{5,4},{6,5},{7,6},{8,7},{9,8},{10,9},{11,1... | collective-permute-start | bytes 4616 | tf_op jit(solution)/shard_map/ppermute | solution.py:19
  49.8 12.7 %collective-permute-start.2 = (bf16[1,2,384]{2,1,0:T(2,128)(2,1)}, bf16[1,2,384]{2,1,0:T(2,128)(2,1)S(1)}, u32[]{:S(2)}, u32[]{:S(2)}) collective-permute-start(bf16[1,2,384]{2,1,0:T(2,128)(2,1)} %get-tuple-element.13), channel_id=1, source_target_pairs={{0,1},{1,2},{2,3},{3,4},{4,5},{5,6},{6,7},{7,8},{8,9},{9,10},{10,1... | collective-permute-start | bytes 4616 | tf_op jit(solution)/shard_map/ppermute | solution.py:16
  52.4 1.0 copy-start.2
  58.2 4.3 copy-start.3
  62.4 2.5 copy-start.7
  68.7 1.4 copy-start.1
  556.0 3.7 copy-start.9
Sparse Core Ops, SparseCore 0:
  68.8 487.1 all-reduce.2
where the time goes:
time: 568 us; the launch traced here: 567 us
  waiting for transfers between devices  483 us (85%)
  starting transfers between devices  24.9 us (4%)
  local copies, waits for them, and re-layouts  21.4 us (4%)
  matrix products  19.3 us (3%)
  between operations  14.4 us (3%)
    psum x1, waiting for transfers between devices, per_device(): conv_grad = lax.psum(tap_grads, ('dp', 'context'))  483 us
    ppermute x3, starting transfers between devices, with_halo(): lax.ppermute(lax.slice_in_dim(block, 0, width, axis=dim), axis, backward)  18.9 us
  transfers between devices with their start and end apart: 7, of which 1 were waited for; matrix products, arithmetic and copies ran while one was open for 6% of the time, Pallas kernels for 0%

commit v1 on v0

--- a/solution.py
+++ b/solution.py
@@ -98,7 +98,9 @@
         preferred_element_type=jnp.float32,
     )
     stem_grad = lax.psum(stem_part, ("dp", "context")).reshape(15, 4, width)
-    conv_grad = lax.psum(tap_grads, ("dp", "context"))
+    conv_grad = tap_grads
+    for over in ("dp", "context"):
+        conv_grad = lax.psum(conv_grad, over)
     return (features, d_pooled, conv_grad, stem_grad)
 
 

time: 568 us -> 1100 us (1.94)
  the two profiles are of different devices: /device:TPU:2 before, /device:TPU:8 now
where the time goes in v1:
time: 1100 us
  waiting for transfers between devices  1030 us (94%)
  matrix products  18.3 us (2%)
  local copies, waits for them, and re-layouts  17.5 us (2%)
  starting transfers between devices  15 us (1%)
  between operations  14.2 us (1%)
    psum x2, waiting for transfers between devices, per_device(): conv_grad = lax.psum(conv_grad, over)  576 us
    psum x1, waiting for transfers between devices, per_device(): stem_grad = lax.psum(stem_part, ('dp', 'context')).reshape(15, 4, width)  453 us
  transfers between devices with their start and end apart: 9, of which 4 were waited for; matrix products, arithmetic and copies ran while one was open for 2% of the time, Pallas kernels for 0%

profile of v1, /device:TPU:8, one launch (start us, length us, event | category | flops | bytes accessed | tf_op | source)
XLA Modules:
  0.0 1099.7 jit_solution(9268334845180871248)
XLA Ops:
  7.2 0.8 select_reduce_fusion
  8.0 0.7 fusion.93
  8.8 1.3 collective-permute-start.1
  10.1 3.0 collective-permute-start
  13.1 0.9 reshape.259
  15.8 1.5 fusion.75
  17.8 2.8 slice.143
  20.6 2.8 slice.142
  23.3 1.8 fusion.29
  25.1 3.4 collective-permute-start.2
  28.6 1.3 collective-permute-start.3
  29.9 1.2 fusion.25
  31.1 1.2 fusion.24
  32.4 1.3 fusion.23
  33.7 1.2 fusion.22
  34.9 1.2 fusion.21
  36.2 0.8 fusion.112
  37.1 4.5 collective-permute-start.5
  41.6 1.3 collective-permute-start.4
  42.9 1.4 fusion.59
  44.4 1.5 collective-permute-done.4
  47.8 1.6 multiply_bitcast_fusion.1
  49.4 0.5 broadcast_in_dim.2
  50.0 2.2 mul.172
  52.2 3.5 fusion.6
  55.7 0.7 reshape.270
  56.5 141.4 %all-reduce.4.cloned.1.call-done = f32[5,384,384]{2,1,0:T(8,128)} async-done(((f32[5,384,384]{2,1,0:T(8,128)}), f32[5,384,384]{2,1,0:T(8,128)}) %all-reduce.4.cloned.1.call-update) | async-done | bytes 2949136 | tf_op jit(solution)/shard_map/psum | solution.py:103
  199.8 1.1 fusion.20
  200.9 453.0 %all-reduce.8.cloned.1.call-done = f32[15,4,384]{2,1,0:T(4,128)} async-done(((f32[15,4,384]{2,1,0:T(4,128)}), f32[15,4,384]{2,1,0:T(4,128)}) %all-reduce.8.cloned.1.call-update) | async-done | bytes 92176 | tf_op jit(solution)/shard_map/psum | solution.py:100
  653.9 435.0 %all-reduce.6.cloned.1.call-done = f32[5,384,384]{2,1,0:T(8,128)} async-done(((f32[5,384,384]{2,1,0:T(8,128)}), f32[5,384,384]{2,1,0:T(8,128)}) %all-reduce.6.cloned.1.call-update) | async-done | bytes 2949136 | tf_op jit(solution)/shard_map/psum | solution.py:103
  1088.9 3.7 copy.41
  1092.5 0.6 copy.42
  (61 shorter events, 6.1 us)
Async XLA Ops:
  7.2 190.7 %all-reduce.4.cloned.1.call-start = ((), (), s32[]{:S(2)}) async-start(), calls=%async_computation | async-start | bytes 5898240 | tf_op jit(solution)/shard_map/psum | solution.py:103
  8.8 5.3 collective-permute-start.1
  10.1 4.0 collective-permute-start
  15.8 1.9 copy-start.7
  23.3 6.6 copy-start.2
  25.1 7.2 copy-start.4
  25.1 4.7 collective-permute-start.2
  28.6 5.1 collective-permute-start.3
  36.1 6.8 copy-start
  36.2 617.8 %all-reduce.8.cloned.1.call-start = ((), (), s32[]{:S(2)}) async-start(), calls=%async_computation.2 | async-start | bytes 184320 | tf_op jit(solution)/shard_map/psum | solution.py:100
  36.2 8.1 copy-start.3
  37.1 9.8 collective-permute-start.5
  41.6 4.3 collective-permute-start.4
  46.8 1.0 copy-start.5
  55.7 142.2 %copy-start.1 = (bf16[5,384,384]{2,1,0:T(8,128)(2,1)S(1)}, bf16[5,384,384]{2,1,0:T(8,128)(2,1)}, u32[]{:S(2)}) copy-start(bf16[5,384,384]{2,1,0:T(8,128)(2,1)} %param.10) | copy-start | bytes 4423684
  56.4 1032.4 %all-reduce.6.cloned.1.call-start = ((), (), s32[]{:S(2)}) async-start(), calls=%async_computation.1 | async-start | bytes 5898240 | tf_op jit(solution)/shard_map/psum | solution.py:103
  197.9 1.0 copy-start.6
  1088.9 3.7 copy-start.8
Sparse Core Ops, SparseCore 0:
  36.3 161.5 all-reduce.3
  203.9 449.9 all-reduce.7
  656.8 431.9 all-reduce.5
